TPU v7x, 32 devices: a whole 2x2x4 slice. The times are simulated.
32 devices in a mesh: groups: 2 (over y), expo: 4 (over z), tile: 4 (over x, core).
Axes of the slice: x: 2, y: 2, z: 4, core: 2. Of those that a mesh axis runs over, the one named last changes fastest.
Arguments:
- template: bfloat16 [8, 64, 4096], P(('groups', 'expo'), 'tile'), parts along dimension 0
- science: bfloat16 [8, 1, 64, 4096], P(('groups', 'expo'), None, 'tile'), parts along dimension 0
- plan: int32 [8], P('groups'), parts along dimension 0, may hold values from 0 to 3, as said below
- orders: int32 [6, 2], replicated, may hold values from 0 to 2
- coadd_weight: float32 [8, 1], P(('groups', 'expo')), parts along dimension 0, may hold values from 0.3 to 3
- intersection: int32 [8, 1], P(('groups', 'expo')), parts along dimension 0, may hold values 0 or 1
Outputs:
- coadd: float32 [2, 64, 4096], P('groups', 'tile', 'expo'), parts along dimension 0
- coeffs: float32 [8, 1, 13], P(('groups', 'expo')), parts along dimension 0
There are 2 independent parts, one for each index of `groups`. A program takes and returns all parts, laid end to end along the dimension named above; an argument that names none is the same for every part. Nothing has to cross between parts.
Inputs may be any that keep to these rules, and one draw needn't show every extreme that they name: `plan`: a permutation of the group's patch indices.
All inputs are finite; a program needn't handle non-finite values. No bound on the sum of `intersection` on one device may be relied on, other than what follows from the above.
Results may differ from a plain program's by a relative error of at most 0.0061.
Values may be sent and summed in bfloat16 or wider, within the bound.
A program may use at most 64 MiB of HBM per device.

v0:
```python
import jax
import jax.numpy as jnp
from jax import lax
from jax.sharding import PartitionSpec as P

HALF = 15
NB = 6
NU = 13
SIGMAS = (0.8, 1.4, 2.2, 3.0, 4.0, 5.5)
RIDGE = 0.05


def broadcast(block, axis, holder):
    block = jnp.where(lax.axis_index(axis) == holder, block, jnp.zeros_like(block))
    return lax.psum(block, axis)


def extended(x, sides, width):
    for axis, dim in sides:
        size, length = (lax.axis_size(axis), x.shape[dim])
        up = [(i, (i + 1) % size) for i in range(size - 1)]
        down = [(j, i) for i, j in up]
        last = lax.slice_in_dim(x, length - width, length, axis=dim)
        first = lax.slice_in_dim(x, 0, width, axis=dim)
        before = lax.ppermute(last, axis, up)
        after = lax.ppermute(first, axis, down)
        x = jnp.concatenate([before, x, after], axis=dim)
    return x


def make_filters(orders):
    taps_pos = jnp.arange(2 * HALF + 1).astype(jnp.float32) - HALF
    row_list = []
    col_list = []
    for basis in range(NB):
        sigma = SIGMAS[basis]
        envelope = jnp.exp(-taps_pos * taps_pos / (2.0 * sigma * sigma))

        def power(order):
            return jnp.where(order == 0, 1.0, jnp.where(order == 1, taps_pos, taps_pos * taps_pos))

        row_filter = envelope * power(orders[basis, 0])
        col_filter = envelope * power(orders[basis, 1])
        row_list.append(row_filter / jnp.sqrt(jnp.sum(row_filter * row_filter)))
        col_list.append(col_filter / jnp.sqrt(jnp.sum(col_filter * col_filter)))
    return (jnp.stack(row_list).astype(jnp.bfloat16), jnp.stack(col_list).astype(jnp.bfloat16))


def band_matrix(filters, out_len, in_len):
    offset = jnp.arange(in_len)[None, :] - jnp.arange(out_len)[:, None]
    taps_idx = jnp.arange(2 * HALF + 1)
    picks = (offset[:, :, None] == taps_idx[None, None, :]).astype(jnp.float32)
    band = jnp.einsum("ijt,kt->kij", picks, filters.astype(jnp.float32))
    return band.astype(jnp.bfloat16)


def per_device(template, science, plan, orders, coadd_weight, intersection):
    row_filters, col_filters = make_filters(orders)
    rows = template.shape[1]
    width = template.shape[2]
    blocks_count = width // 128
    steps_count = science.shape[1]
    row_band = band_matrix(row_filters, rows, rows + 2 * HALF)
    col_band = jnp.transpose(band_matrix(col_filters, 128, 128 + 2 * HALF), (0, 2, 1))
    column_pos = 2.0 * (jnp.arange(width).astype(jnp.float32) + 0.5) / width - 1.0
    pieces = []
    fitted = []
    for step in range(steps_count):
        owner_index = plan[step]
        received = broadcast(template[0], "expo", owner_index)
        padded = extended(received, (("tile", 0),), HALF)
        rowconv = jnp.einsum(
            "kij,jw->kiw", row_band, padded, preferred_element_type=jnp.float32
        ).astype(jnp.bfloat16)
        blocks = rowconv.reshape(NB, rows, blocks_count, 128)
        empty_rim = jnp.zeros((NB, rows, 1, HALF), jnp.bfloat16)
        previous = jnp.concatenate([empty_rim, blocks[:, :, :-1, 128 - HALF :]], axis=2)
        following = jnp.concatenate([blocks[:, :, 1:, :HALF], empty_rim], axis=2)
        window = jnp.concatenate([previous, blocks, following], axis=3)
        conv = jnp.einsum("krbj,kjc->krbc", window, col_band, preferred_element_type=jnp.float32)
        conv = conv.reshape(NB, rows, width)
        fields = jnp.concatenate(
            [conv, conv * column_pos, jnp.ones((1, rows, width), jnp.float32)], axis=0
        )
        fields = fields.reshape(NU, rows * width)
        exposure_image = science[0, step].astype(jnp.float32).reshape(rows * width)
        normal_local = jnp.dot(fields, fields.T, precision=lax.Precision.HIGHEST)
        project_local = jnp.dot(fields, exposure_image, precision=lax.Precision.HIGHEST)
        normal_matrix, projections = lax.psum((normal_local, project_local), "tile")
        normal_matrix = normal_matrix + RIDGE * (jnp.trace(normal_matrix) / NU) * jnp.eye(
            NU, dtype=jnp.float32
        )
        factor = jnp.linalg.cholesky(normal_matrix)
        coeffs = jax.scipy.linalg.cho_solve((factor, True), projections)
        model = jnp.dot(coeffs, fields, precision=lax.Precision.HIGHEST)
        difference = exposure_image - model
        weight_now = coadd_weight[0, step] * intersection[0, step].astype(jnp.float32)
        pieces.append((weight_now * difference).reshape(rows, width))
        fitted.append(coeffs)
    weighted = jnp.stack(pieces)
    received_parts = lax.all_to_all(weighted[None], "expo", split_axis=3, concat_axis=0, tiled=True)
    coadd = jnp.sum(received_parts, axis=0)
    return (coadd, jnp.stack(fitted)[None])


def solution(mesh):
    return jax.shard_map(
        per_device,
        mesh=mesh,
        in_specs=(
            P(("groups", "expo"), "tile", None),
            P(("groups", "expo"), None, "tile", None),
            P("groups"),
            P(),
            P(("groups", "expo"), None),
            P(("groups", "expo"), None),
        ),
        out_specs=(P("groups", "tile", "expo"), P(("groups", "expo"), None, None)),
        check_vma=False,
    )
```

profile of v0, /device:TPU:0, one launch (start us, length us, event | category | flops | bytes accessed | tf_op | source)
XLA Modules:
  0.0 144.0 jit_solution(105199897231821041)
XLA Ops:
  8.6 1.8 %fusion.124 = (s32[1,1]{0,1:T(1,128)}, s32[1,1]{0,1:T(1,128)}, s32[1,1]{0,1:T(1,128)}, s32[1,1]{0,1:T(1,128)}, s32[1,1]{0,1:T(1,128)}, /*index=5*/s32[1,1]{0,1:T...) fusion(s32[6,2]{0,1:T(2,128)} %param.9), kind=kLoop, calls=%fused_computation.211 | loop fusion | bytes 96 | tf_op jit(solution)/shard_map/slice | solution.py:43
  42.9 1.8 %copy.41 = bf16[1,1,16,4096]{3,1,2,0:T(2,128)(2,1)} copy(bf16[1,1,16,4096]{3,2,1,0:T(8,128)(2,1)} %param.7) | data formatting | bytes 262144
  46.4 1.4 all-reduce.5.cloned.1.call-done
  47.8 1.0 fusion.123
  48.8 1.3 collective-permute-start
  50.1 1.3 collective-permute-start.1
  52.0 3.2 %collective-permute-done.1 = bf16[15,4096]{1,0:T(8,128)(2,1)S(1)} collective-permute-done((bf16[15,4096]{1,0:T(8,128)(2,1)S(1)}, bf16[15,4096]{1,0:T(8,128)(2,1)S(1)}, u32[]{:S(2)}, u32[]{:S(2)}) %collective-permute-start.1) | collective-permute-done | bytes 122912 | tf_op jit(solution)/shard_map/ppermute | solution.py:26
  55.2 1.3 convolution_convert_fusion
  57.2 1.5 %fusion.10 = f32[6,16,32,128]{3,2,1,0:T(8,128)S(1)} fusion(bf16[6,16,31,15]{3,2,1,0:T(8,128)(2,1)S(1)} %get-tuple-element.9, bf16[6,16,31,15]{3,2,1,0:T(8,128)(2,1)S(1)} %get-tuple-element.8, bf16[6,16,32,128]{3,2,1,0:T(8,128)(2,1)S(1)} %bitcast.105, bf16[6,128,158,1]{1,0,2,3:T(8,128)(2,1)S(1)} %fusion.21), kind=kOutput, calls=%fused_computation.17 | convolution fusion | flops 129110016 | bytes 2780544 | tf_op jit(solution)/shard_map/krbj,kjc->krbc/dot_general | solution.py:80
  60.1 6.5 %fusion.22 = f32[13,13]{1,0:T(8,128)S(1)} fusion(f32[13,16,4096]{2,1,0:T(8,128)S(1)} %maximum_maximum_fusion.1), kind=kOutput, calls=%fused_computation.28 | convolution fusion | flops 132907008 | bytes 3408548 | tf_op jit(solution)/shard_map/dot_general | solution.py:87
  66.6 1.0 copy.53
  67.6 1.0 broadcast_multiply_fusion
  68.9 1.0 copy-done.1
  69.9 3.3 %fusion.25 = f32[13]{0:T(128)S(1)} fusion(bf16[65536,1]{0,1:T(2,128)(2,1)S(1)} %bitcast.112, f32[6,65536]{1,0:T(8,128)S(1)} %broadcast_multiply_fusion, f32[6,65536]{1,0:T(8,128)S(1)} %bitcast.100, f32[13]{0:T(128)S(1)} %copy-done.4), kind=kOutput, calls=%fused_computation.30 | convolution fusion | flops 11927552 | bytes 3276904 | tf_op jit(solution)/shard_map/dot_general | solution.py:88
  73.2 9.7 %all-reduce.2 = (f32[13,13]{1,0:T(8,128)S(1)}, f32[13]{0:T(128)S(1)}) all-reduce(f32[13,13]{1,0:T(8,128)S(1)} %fusion.22, f32[13]{0:T(128)S(1)} %fusion.25), channel_id=1, replica_groups=mesh['groups'=2,'expo'=4,'tile'=4] {'tile'}, use_global_device_ids=true, to_apply=%region_13.14 | all-reduce | flops 182 | bytes 1456 | tf_op jit(solution)/shard_map/psum | solution.py:89
  84.3 1.2 cholesky.17
  86.8 1.0 custom-call.10
  88.1 5.0 %fusion.2 = f32[1,65536]{1,0:T(1,128)S(1)} fusion(f32[6,65536]{1,0:T(8,128)} %copy-done.1, f32[6,65536]{1,0:T(8,128)} %bitcast.101, f32[13]{0:T(128)S(1)} %copy-done.5, f32[1,13]{1,0:T(1,128)S(1)} %fusion.35), kind=kOutput, calls=%fused_computation.5 | convolution fusion | flops 11927552 | bytes 3407976 | tf_op jit(solution)/shard_map/dot_general | solution.py:95
  93.2 2.5 %copy.32 = f32[1,1,16,4096]{2,1,0,3:T(1,128)S(1)} copy(f32[1,1,16,4096]{3,2,1,0:T(8,128)S(1)} %broadcast_in_dim_stack_reshape.3) | data formatting | bytes 524288 | tf_op jit(solution)/shard_map/broadcast_in_dim;stack;reshape | solution.py:101
  96.2 19.4 %reduce.10 = f32[4096,16]{1,0:T(8,128)} reduce(f32[4096,1,1,16]{3,2,1,0:T(1,128)S(1)} %bitcast.102, f32[]{:T(128)} %broadcast.809), dimensions={1,2}, to_apply=%bitcast.92.reduce_sub_computation | reduce | bytes 524292
  115.6 2.3 %reshape.354 = f32[4,1,16384]{2,1,0:T(1,128)S(1)} reshape(f32[4096,16]{1,0:T(8,128)} %reduce.10) | data formatting | bytes 524288
  117.9 13.2 %all_to_all.12 = f32[4,1,16384]{2,1,0:T(1,128)S(1)} all-to-all(f32[4,1,16384]{2,1,0:T(1,128)S(1)} %reshape.354), channel_id=1, replica_groups=mesh['groups'=2,'expo'=4,'tile'=4] {'expo'}, dimensions={0} | all-to-all | bytes 524288 | tf_op jit(solution)/shard_map/all_to_all | solution.py:101
  131.0 1.4 reduce.11
  132.4 3.7 %reshape.355 = f32[4096,1,1,16]{3,2,1,0:T(1,128)S(1)} reshape(f32[4,16384]{1,0:T(4,128)S(1)} %reduce.11) | data formatting | bytes 524288
  (63 shorter events, 16.8 us)
Async XLA Ops:
  7.2 40.6 %all-reduce.5.cloned.1.call-start = ((), (), s32[]{:S(2)}) async-start(), calls=%async_computation.1 | async-start | bytes 262144 | tf_op jit(solution)/shard_map/psum | solution.py:15
  48.8 3.1 %collective-permute-start = (bf16[15,4096]{1,0:T(8,128)(2,1)S(1)}, bf16[15,4096]{1,0:T(8,128)(2,1)S(1)}, u32[]{:S(2)}, u32[]{:S(2)}) collective-permute-start(bf16[15,4096]{1,0:T(8,128)(2,1)S(1)} %get-tuple-element.10), channel_id=1, source_target_pairs={{0,1},{1,2},{2,3},{4,5},{5,6},{6,7},{8,9},{9,10},{10,11},{12,13},{... | collective-permute-start | bytes 368648 | tf_op jit(solution)/shard_map/ppermute | solution.py:25
  50.1 5.1 %collective-permute-start.1 = (bf16[15,4096]{1,0:T(8,128)(2,1)S(1)}, bf16[15,4096]{1,0:T(8,128)(2,1)S(1)}, u32[]{:S(2)}, u32[]{:S(2)}) collective-permute-start(bf16[15,4096]{1,0:T(8,128)(2,1)S(1)} %get-tuple-element.11), channel_id=1, source_target_pairs={{1,0},{2,1},{3,2},{5,4},{6,5},{7,6},{9,8},{10,9},{11,10},{13,12},{... | collective-permute-start | bytes 368648 | tf_op jit(solution)/shard_map/ppermute | solution.py:26
  59.0 0.7 copy-start.4
  67.6 1.3 copy-start
  67.6 2.3 %copy-start.2 = (bf16[1,1,16,4096]{3,1,2,0:T(2,128)(2,1)S(1)}, bf16[1,1,16,4096]{3,1,2,0:T(2,128)(2,1)}, u32[]{:S(2)}) copy-start(bf16[1,1,16,4096]{3,1,2,0:T(2,128)(2,1)} %copy.41) | copy-start | bytes 393220
  68.6 1.4 copy-start.1
  69.9 18.1 %copy-start.5 = (f32[13]{0:T(128)S(1)}, f32[13]{0:T(128)}, u32[]{:S(2)}) copy-start(f32[13]{0:T(128)} %pad.7.clone) | copy-start | bytes 160
  88.1 5.0 %copy-start.3 = (f32[1,13]{1,0:T(1,128)}, f32[1,13]{1,0:T(1,128)S(1)}, u32[]{:S(2)}) copy-start(f32[1,13]{1,0:T(1,128)S(1)} %fusion.35) | copy-start | bytes 160
Sparse Core Ops, SparseCore 0:
  10.3 37.4 all-reduce.4
where the time goes:
time: 145 us; the launch traced here: 144 us
  between operations  40.4 us (28%)
  other arithmetic  34.7 us (24%)
  blocking collectives  22.8 us (16%)
  local copies, waits for them, and re-layouts  20.1 us (14%)
  matrix products  18.6 us (13%)
  waiting for transfers between devices  4.66 us (3%)
  starting transfers between devices  2.63 us (2%)
    unnamed x1, other arithmetic  19.4 us
    all_to_all x1, blocking collectives, per_device(): lax.all_to_all(weighted[None], 'expo', split_axis=3, concat_axis=0, tiled...  13.2 us
    unnamed x22, local copies, waits for them, and re-layouts  13.1 us
    psum x1, blocking collectives, per_device(): normal_matrix, projections = lax.psum((normal_local, project_local), 'tile')  9.66 us
    dot_general x1, matrix products, per_device(): normal_local = jnp.dot(fields, fields.T, precision=lax.Precision.HIGHEST)  6.53 us
    dot_general x1, matrix products, per_device(): model = jnp.dot(coeffs, fields, precision=lax.Precision.HIGHEST)  5.02 us
    reduce_sum x6, other arithmetic, make_filters(): col_list.append(col_filter / jnp.sqrt(jnp.sum(col_filter * col_filter)))  3.69 us
    reduce_sum x6, other arithmetic, make_filters(): row_list.append(row_filter / jnp.sqrt(jnp.sum(row_filter * row_filter)))  3.69 us
  transfers between devices with their start and end apart: 3, of which 2 were waited for; matrix products, arithmetic and copies ran while one was open for 9% of the time, Pallas kernels for 0%

commit v1 on v0

--- a/solution.py
+++ b/solution.py
@@ -98,7 +98,12 @@
         pieces.append((weight_now * difference).reshape(rows, width))
         fitted.append(coeffs)
     weighted = jnp.stack(pieces)
-    received_parts = lax.all_to_all(weighted[None], "expo", split_axis=3, concat_axis=0, tiled=True)
+    received_parts = jnp.concatenate(
+        lax.all_to_all(
+            jnp.stack(jnp.split(weighted[None], lax.axis_size("expo"), axis=3)), "expo", 0, 0
+        ),
+        axis=0,
+    )
     coadd = jnp.sum(received_parts, axis=0)
     return (coadd, jnp.stack(fitted)[None])
 

time: 145 us -> 115 us (0.79)
  other arithmetic: 34.7 us -> 14.8 us
  local copies, waits for them, and re-layouts: 20.1 us -> 10.3 us
    unnamed x1 -> x0, other arithmetic: 19.4 us -> none
    unnamed x22 -> x18, local copies, waits for them, and re-layouts: 13.1 us -> 5.83 us
    another operation x2 -> x1, local copies, waits for them, and re-layouts: 2.53 us -> 0.05 us  [per_device(): weighted[None]]
  transfers between devices with their start and end apart: 3 -> 3, of which waited for: 2 -> 2; matrix products, arithmetic and copies ran while one was open for 9% -> 12% of each run, Pallas kernels for 0% -> 0%
where the time goes in v1:
time: 115 us; the launch traced here: 114 us
  between operations  40.6 us (35%)
  blocking collectives  22.8 us (20%)
  matrix products  18.5 us (16%)
  other arithmetic  14.8 us (13%)
  local copies, waits for them, and re-layouts  10.3 us (9%)
  waiting for transfers between devices  4.35 us (4%)
  starting transfers between devices  3.01 us (3%)
    all_to_all x1, blocking collectives, per_device(): lax.all_to_all(jnp.stack(jnp.split(weighted[None], lax.axis_size('expo'),...  13.2 us
    psum x1, blocking collectives, per_device(): normal_matrix, projections = lax.psum((normal_local, project_local), 'tile')  9.66 us
    dot_general x1, matrix products, per_device(): normal_local = jnp.dot(fields, fields.T, precision=lax.Precision.HIGHEST)  6.53 us
    unnamed x18, local copies, waits for them, and re-layouts  5.83 us
    dot_general x1, matrix products, per_device(): model = jnp.dot(coeffs, fields, precision=lax.Precision.HIGHEST)  5.02 us
    reduce_sum x6, other arithmetic, make_filters(): col_list.append(col_filter / jnp.sqrt(jnp.sum(col_filter * col_filter)))  3.69 us
    reduce_sum x6, other arithmetic, make_filters(): row_list.append(row_filter / jnp.sqrt(jnp.sum(row_filter * row_filter)))  3.69 us
    ppermute x1, waiting for transfers between devices, extended(): after = lax.ppermute(first, axis, down)  3.59 us
  transfers between devices with their start and end apart: 3, of which 2 were waited for; matrix products, arithmetic and copies ran while one was open for 12% of the time, Pallas kernels for 0%

profile of v1, /device:TPU:0, one launch (start us, length us, event | category | flops | bytes accessed | tf_op | source)
XLA Modules:
  0.0 114.4 jit_solution(10389166510827092128)
XLA Ops:
  7.9 0.7 select_bitcast_fusion
  8.6 1.8 %fusion.128 = (s32[1,1]{0,1:T(1,128)}, s32[1,1]{0,1:T(1,128)}, s32[1,1]{0,1:T(1,128)}, s32[1,1]{0,1:T(1,128)}, s32[1,1]{0,1:T(1,128)}, /*index=5*/s32[1,1]{0,1:T...) fusion(s32[6,2]{0,1:T(2,128)} %param.9), kind=kLoop, calls=%fused_computation.216 | loop fusion | bytes 96 | tf_op jit(solution)/shard_map/slice | solution.py:43
  42.8 1.8 %copy.27 = bf16[1,1,16,4096]{3,1,2,0:T(2,128)(2,1)} copy(bf16[1,1,16,4096]{3,2,1,0:T(8,128)(2,1)} %param.7) | data formatting | bytes 262144
  44.6 0.9 copy.23
  46.9 0.7 all-reduce.5.cloned.1.call-done
  47.7 1.0 fusion.127
  48.7 1.7 %collective-permute-start = (bf16[15,4096]{1,0:T(8,128)(2,1)S(1)}, bf16[15,4096]{1,0:T(8,128)(2,1)S(1)}, u32[]{:S(2)}, u32[]{:S(2)}) collective-permute-start(bf16[15,4096]{1,0:T(8,128)(2,1)S(1)} %get-tuple-element.10), channel_id=1, source_target_pairs={{0,1},{1,2},{2,3},{4,5},{5,6},{6,7},{8,9},{9,10},{10,11},{12,13},{... | collective-permute-start | bytes 368648 | tf_op jit(solution)/shard_map/ppermute | solution.py:25
  50.4 1.3 %collective-permute-start.1 = (bf16[15,4096]{1,0:T(8,128)(2,1)S(1)}, bf16[15,4096]{1,0:T(8,128)(2,1)S(1)}, u32[]{:S(2)}, u32[]{:S(2)}) collective-permute-start(bf16[15,4096]{1,0:T(8,128)(2,1)S(1)} %get-tuple-element.11), channel_id=1, source_target_pairs={{1,0},{2,1},{3,2},{5,4},{6,5},{7,6},{9,8},{10,9},{11,10},{13,12},{... | collective-permute-start | bytes 368648 | tf_op jit(solution)/shard_map/ppermute | solution.py:26
  52.1 3.6 %collective-permute-done.1 = bf16[15,4096]{1,0:T(8,128)(2,1)S(1)} collective-permute-done((bf16[15,4096]{1,0:T(8,128)(2,1)S(1)}, bf16[15,4096]{1,0:T(8,128)(2,1)S(1)}, u32[]{:S(2)}, u32[]{:S(2)}) %collective-permute-start.1) | collective-permute-done | bytes 122912 | tf_op jit(solution)/shard_map/ppermute | solution.py:26
  55.7 1.3 %convolution_convert_fusion = bf16[6,16,4096]{2,1,0:T(8,128)(2,1)S(1)} fusion(bf16[15,4096]{1,0:T(8,128)(2,1)S(1)} %collective-permute-done.1, bf16[16,4096]{1,0:T(8,128)(2,1)} %all-reduce.5.cloned.1.call-done, bf16[15,4096]{1,0:T(8,128)(2,1)S(1)} %collective-permute-done, bf16[6,16,46]{2,0,1:T(8,128)(2,1)S(1)} %convolution_convert_fusion.1), kind=kOutput, calls=%fused_computation | convolution fusion | flops 37699584 | bytes 1172096 | tf_op jit(solution)/shard_map/kij,jw->kiw/dot_general | solution.py:72
  57.7 1.5 %fusion.11 = f32[6,16,32,128]{3,2,1,0:T(8,128)S(1)} fusion(bf16[6,16,31,15]{3,2,1,0:T(8,128)(2,1)S(1)} %get-tuple-element.5, bf16[6,16,31,15]{3,2,1,0:T(8,128)(2,1)S(1)} %get-tuple-element.4, bf16[6,16,32,128]{3,2,1,0:T(8,128)(2,1)S(1)} %bitcast.108, bf16[6,128,158,1]{1,0,2,3:T(8,128)(2,1)S(1)} %fusion.23), kind=kOutput, calls=%fused_computation.18 | convolution fusion | flops 129110016 | bytes 2780544 | tf_op jit(solution)/shard_map/krbj,kjc->krbc/dot_general | solution.py:80
  60.6 6.5 %fusion.26 = f32[13,13]{1,0:T(8,128)S(1)} fusion(f32[13,16,4096]{2,1,0:T(8,128)S(1)} %maximum_maximum_fusion.1), kind=kOutput, calls=%fused_computation.28 | convolution fusion | flops 132907008 | bytes 3408548 | tf_op jit(solution)/shard_map/dot_general | solution.py:87
  67.1 1.0 copy.45
  68.1 1.0 broadcast_multiply_fusion
  69.4 1.0 copy-done.1
  70.4 3.3 %fusion.29 = f32[13]{0:T(128)S(1)} fusion(bf16[65536,1]{0,1:T(2,128)(2,1)S(1)} %bitcast.114, f32[6,65536]{1,0:T(8,128)S(1)} %broadcast_multiply_fusion, f32[6,65536]{1,0:T(8,128)S(1)} %bitcast.105, f32[13]{0:T(128)S(1)} %copy-done.4), kind=kOutput, calls=%fused_computation.30 | convolution fusion | flops 11927552 | bytes 3276904 | tf_op jit(solution)/shard_map/dot_general | solution.py:88
  73.7 9.7 %all-reduce.2 = (f32[13,13]{1,0:T(8,128)S(1)}, f32[13]{0:T(128)S(1)}) all-reduce(f32[13,13]{1,0:T(8,128)S(1)} %fusion.26, f32[13]{0:T(128)S(1)} %fusion.29), channel_id=1, replica_groups=mesh['groups'=2,'expo'=4,'tile'=4] {'tile'}, use_global_device_ids=true, to_apply=%region_13.14 | all-reduce | flops 182 | bytes 1456 | tf_op jit(solution)/shard_map/psum | solution.py:89
  84.8 1.2 %cholesky.17 = f32[13,13]{1,0:T(8,128)S(1)} custom-call(f32[13,13]{1,0:T(8,128)S(1)} %fusion.42), custom_call_target="Cholesky" | custom-call | tf_op jit(solution)/shard_map/jit(cholesky)/cholesky | solution.py:93
  86.0 0.6 compare_reduce_fusion
  86.6 0.6 fusion.38
  87.3 1.0 custom-call.10
  88.6 5.0 %fusion.2 = f32[1,65536]{1,0:T(1,128)S(1)} fusion(f32[6,65536]{1,0:T(8,128)} %copy-done.1, f32[6,65536]{1,0:T(8,128)} %bitcast.106, f32[13]{0:T(128)S(1)} %copy-done.5, f32[1,13]{1,0:T(1,128)S(1)} %fusion.39), kind=kOutput, calls=%fused_computation.5 | convolution fusion | flops 11927552 | bytes 3407976 | tf_op jit(solution)/shard_map/dot_general | solution.py:95
  93.8 13.2 %all_to_all.5 = f32[4,1,1,16,1024]{4,3,2,1,0:T(8,128)S(1)} all-to-all(f32[4,1,1,16,1024]{4,3,2,1,0:T(8,128)S(1)} %pad_maximum_fusion), channel_id=1, replica_groups=mesh['groups'=2,'expo'=4,'tile'=4] {'expo'}, dimensions={0} | all-to-all | bytes 524288 | tf_op jit(solution)/shard_map/all_to_all | solution.py:102
  106.9 0.6 reduce_sum.142
  (59 shorter events, 12.7 us)
Async XLA Ops:
  7.2 40.5 %all-reduce.5.cloned.1.call-start = ((), (), s32[]{:S(2)}) async-start(), calls=%async_computation.1 | async-start | bytes 262144 | tf_op jit(solution)/shard_map/psum | solution.py:15
  48.7 3.4 %collective-permute-start = (bf16[15,4096]{1,0:T(8,128)(2,1)S(1)}, bf16[15,4096]{1,0:T(8,128)(2,1)S(1)}, u32[]{:S(2)}, u32[]{:S(2)}) collective-permute-start(bf16[15,4096]{1,0:T(8,128)(2,1)S(1)} %get-tuple-element.10), channel_id=1, source_target_pairs={{0,1},{1,2},{2,3},{4,5},{5,6},{6,7},{8,9},{9,10},{10,11},{12,13},{... | collective-permute-start | bytes 368648 | tf_op jit(solution)/shard_map/ppermute | solution.py:25
  50.4 5.3 %collective-permute-start.1 = (bf16[15,4096]{1,0:T(8,128)(2,1)S(1)}, bf16[15,4096]{1,0:T(8,128)(2,1)S(1)}, u32[]{:S(2)}, u32[]{:S(2)}) collective-permute-start(bf16[15,4096]{1,0:T(8,128)(2,1)S(1)} %get-tuple-element.11), channel_id=1, source_target_pairs={{1,0},{2,1},{3,2},{5,4},{6,5},{7,6},{9,8},{10,9},{11,10},{13,12},{... | collective-permute-start | bytes 368648 | tf_op jit(solution)/shard_map/ppermute | solution.py:26
  59.5 0.7 copy-start.4
  68.1 1.3 %copy-start = (f32[1,6,512,128]{3,1,2,0:T(8,128)}, f32[1,6,512,128]{3,1,2,0:T(8,128)S(1)}, u32[]{:S(2)}) copy-start(f32[1,6,512,128]{3,1,2,0:T(8,128)S(1)} %copy.45) | copy-start | bytes 4718596
  68.1 2.3 %copy-start.2 = (bf16[1,1,16,4096]{3,1,2,0:T(2,128)(2,1)S(1)}, bf16[1,1,16,4096]{3,1,2,0:T(2,128)(2,1)}, u32[]{:S(2)}) copy-start(bf16[1,1,16,4096]{3,1,2,0:T(2,128)(2,1)} %copy.27) | copy-start | bytes 393220
  69.1 1.4 %copy-start.1 = (f32[6,65536]{1,0:T(8,128)}, f32[6,65536]{1,0:T(8,128)S(1)}, u32[]{:S(2)}) copy-start(f32[6,65536]{1,0:T(8,128)S(1)} %broadcast_multiply_fusion) | copy-start | bytes 4718596
  70.4 18.1 %copy-start.5 = (f32[13]{0:T(128)S(1)}, f32[13]{0:T(128)}, u32[]{:S(2)}) copy-start(f32[13]{0:T(128)} %pad.11.clone) | copy-start | bytes 160
  88.6 5.1 %copy-start.3 = (f32[1,13]{1,0:T(1,128)}, f32[1,13]{1,0:T(1,128)S(1)}, u32[]{:S(2)}) copy-start(f32[1,13]{1,0:T(1,128)S(1)} %fusion.39) | copy-start | bytes 160
Sparse Core Ops, SparseCore 0:
  10.3 37.3 all-reduce.4
